TPU v7x, 32 devices: a whole 2x2x4 slice. The times are simulated.
32 devices in a mesh: seq: 8 (over z, x), head: 4 (over y, core).
Axes of the slice: x: 2, y: 2, z: 4, core: 2. Of those that a mesh axis runs over, the one named last changes fastest.
Arguments:
- queries: bfloat16 [4096, 5120], P('seq', 'head'), may hold values from -13 to 13, as said below
- keys: bfloat16 [4096, 1024], P('seq', 'head'), may hold values from -13 to 13, as said below
- values: bfloat16 [4096, 1024], P('seq', 'head'), may hold values from -6 to 6
- out_weight: bfloat16 [5120, 2560], P('head', 'seq'), may hold values from -0.078125 to 0.078125
- d_proj: bfloat16 [4096, 2560], P('seq', 'head'), may hold values from -6 to 6
- block_section: int32 [32], replicated, may hold values from 0 to 3, as said below
- section_parent: int32 [4], replicated, may hold values from -1 to 2, as said below
- xref_owner: int32 [384, 1], P('seq'), may hold values from 0 to 7; in each aligned block of 48 rows (0 to 47, 48 to 95, ...) at most 6 rows name the same one
- xref_block: int32 [32, 12], P('seq'), may hold values from 0 to 3
- xref_valid: int32 [32, 12], P('seq'), may hold values 0 or 1
Outputs:
- projected: bfloat16 [4096, 2560], P('seq', 'head')
- d_queries: bfloat16 [4096, 5120], P('seq', 'head')
- d_keys: bfloat16 [4096, 1024], P('seq', 'head')
- d_values: bfloat16 [4096, 1024], P('seq', 'head')
Inputs may be any that keep to these rules, and one draw needn't show every extreme that they name: `queries`: entries of order one; a few rows of larger norm. `keys`: entries of order one; a few rows of larger norm. section_parent[s] is an earlier section for s > 0, and section_parent[0] = -1. `block_section`: sections are runs of consecutive blocks, 2 to 14 blocks each, some section exactly 14; no section begins at a block whose index is a positive multiple of 4. `xref_owner`: among the 48 rows of one device, no owner is named more than 6 times; some owner exactly 6 times.
All inputs are finite; a program needn't handle non-finite values. No bound on the sum of `xref_valid` on one device may be relied on, other than what follows from the above.
Results may differ from a plain program's by a relative error of at most 0.015.
The roundings to bfloat16 on the way count: a program that leaves them out, or rounds other values in their place, can miss the bound.
Values may be sent and summed in bfloat16 or wider, within the bound.
No kernel may reach another device: no remote copies, remote signals or barrier semaphores. Data moves between devices by JAX's collectives and lax.ppermute only.
A program may use at most 192 MiB of HBM per device.

v0:
```python
import jax
import jax.numpy as jnp
from jax import lax
from jax.sharding import PartitionSpec as P

HEAD_DIMENSION = 128
BLK = 128
LOOK = 4
ANC = 2
XREF = 12
neg_large = -1e30


def passed_along(block, axis, distance):
    devices = range(lax.axis_size(axis))
    route = [(i - distance, i) for i in devices if i - distance in devices]
    return lax.ppermute(block, axis, route)


def query_layout(block, kv_heads):
    row_count = block.shape[0]
    group_size = block.shape[1] // (HEAD_DIMENSION * kv_heads)
    return block.reshape(row_count, kv_heads, group_size, HEAD_DIMENSION)


def key_layout(key_set, kv_heads):
    num_blocks, row_count, key_value_width = key_set.shape
    return key_set.reshape(num_blocks * row_count, kv_heads, HEAD_DIMENSION)


def softmax_weights(scores, allowed):
    masked = jnp.where(allowed, scores, neg_large)
    row_max = jnp.max(masked, axis=-1, keepdims=True)
    exponent = jnp.where(allowed, jnp.exp(masked - row_max), 0.0)
    return exponent / jnp.sum(exponent, axis=-1, keepdims=True)


def product(form, left, right):
    return jnp.einsum(form, left, right, preferred_element_type=jnp.float32)


def forward_block(query_block, key_set, value_set, allowed):
    kv_heads = key_set.shape[2] // HEAD_DIMENSION
    scaling = HEAD_DIMENSION ** (-0.5)
    query_heads = query_layout(query_block, kv_heads)
    key_heads = key_layout(key_set, kv_heads)
    value_heads = key_layout(value_set, kv_heads)
    scores = product("qcgd,kcd->cqgk", query_heads, key_heads) * scaling
    weights = softmax_weights(scores, allowed[None, :, None, :])
    output = product("cqgk,kcd->qcgd", weights.astype(jnp.bfloat16), value_heads)
    return output.reshape(query_block.shape[0], -1).astype(jnp.bfloat16)


def backward_block(query_block, key_set, value_set, allowed, attn, d_attn):
    kv_heads = key_set.shape[2] // HEAD_DIMENSION
    scaling = HEAD_DIMENSION ** (-0.5)
    num_blocks = key_set.shape[0]
    row_count = query_block.shape[0]
    query_heads = query_layout(query_block, kv_heads)
    key_heads = key_layout(key_set, kv_heads)
    value_heads = key_layout(value_set, kv_heads)
    scores = product("qcgd,kcd->cqgk", query_heads, key_heads) * scaling
    weights = softmax_weights(scores, allowed[None, :, None, :])
    light = weights.astype(jnp.bfloat16)
    grad_heads = query_layout(d_attn, kv_heads)
    attn_heads = query_layout(attn, kv_heads)
    delta = jnp.einsum(
        "qcgd,qcgd->cqg", grad_heads.astype(jnp.float32), attn_heads.astype(jnp.float32)
    )[..., None]
    d_weights = product("qcgd,kcd->cqgk", grad_heads, value_heads)
    d_scores = (weights * (d_weights - delta) * scaling).astype(jnp.bfloat16)
    grad_query = product("cqgk,kcd->qcgd", d_scores, key_heads)
    key_terms = product("cqgk,qcgd->kcd", d_scores, query_heads)
    value_terms = product("cqgk,qcgd->kcd", light, grad_heads)
    return (
        grad_query.reshape(row_count, -1).astype(jnp.bfloat16),
        key_terms.reshape(num_blocks, -1),
        value_terms.reshape(num_blocks, -1),
    )


def run_forward(operands):
    return forward_block(operands[0], operands[1], operands[2], operands[3])


def run_backward(operands):
    return backward_block(
        operands[0], operands[1], operands[2], operands[3], operands[4], operands[5]
    )


def on_device(
    queries,
    keys,
    values,
    out_weight,
    d_proj,
    block_section,
    section_parent,
    xref_owner,
    xref_block,
    xref_valid,
):
    seq_count = lax.axis_size("seq")
    seq_rank = lax.axis_index("seq")
    tok_local = queries.shape[0]
    blk_count = tok_local // BLK
    key_value_width = keys.shape[1]
    blk_width = BLK * key_value_width
    sections = section_parent.shape[0]
    behind = LOOK - 1
    key_count = LOOK + ANC + XREF
    first_blk = seq_rank * blk_count
    key_flat = keys.reshape(blk_count, blk_width)
    value_flat = values.reshape(blk_count, blk_width)
    section_ids = jnp.arange(sections, dtype=jnp.int32)
    my_sec = lax.dynamic_slice_in_dim(block_section, first_blk, blk_count)
    counts = jnp.sum((block_section[:, None] == section_ids[None, :]).astype(jnp.float32), axis=0)
    root_counts = jnp.sqrt(counts)
    mine = (section_ids[:, None] == my_sec[None, :]).astype(jnp.float32)
    chain = [my_sec]
    prior = chain[-1]
    chain.append(
        jnp.where(
            prior >= 0,
            jnp.sum(
                jnp.where(prior[:, None] == section_ids[None, :], section_parent[None, :], 0),
                axis=1,
            ),
            -1,
        )
    )
    ancestors = jnp.stack(chain, axis=1).reshape(-1)
    chosen_up = ancestors[:, None] == section_ids[None, :]
    prev_keys, prev_values = passed_along(
        (keys[tok_local - behind * BLK :], values[tok_local - behind * BLK :]), "seq", 1
    )
    extended_keys = jnp.concatenate([prev_keys, keys], axis=0).reshape(
        blk_count + behind, BLK, key_value_width
    )
    extended_values = jnp.concatenate([prev_values, values], axis=0).reshape(
        blk_count + behind, BLK, key_value_width
    )
    mine_light = mine.astype(jnp.bfloat16)
    part_keys = (
        jnp.dot(mine_light, key_flat, preferred_element_type=jnp.float32) / root_counts[:, None]
    )
    part_values = (
        jnp.dot(mine_light, value_flat, preferred_element_type=jnp.float32) / root_counts[:, None]
    )
    total_keys, total_values = (
        lax.psum(part_keys.astype(jnp.bfloat16), "seq").astype(jnp.float32),
        lax.psum(part_values.astype(jnp.bfloat16), "seq").astype(jnp.float32),
    )
    summary_keys = total_keys.astype(jnp.bfloat16)
    summary_values = total_values.astype(jnp.bfloat16)
    chosen_light = chosen_up.astype(jnp.bfloat16)
    up_keys = (
        jnp.dot(chosen_light, summary_keys, preferred_element_type=jnp.float32)
        .astype(jnp.bfloat16)
        .reshape(blk_count, ANC, BLK, key_value_width)
    )
    up_values = (
        jnp.dot(chosen_light, summary_values, preferred_element_type=jnp.float32)
        .astype(jnp.bfloat16)
        .reshape(blk_count, ANC, BLK, key_value_width)
    )
    owners = xref_owner.reshape(-1)
    wanted = xref_block.reshape(-1)
    slot_total = owners.shape[0]
    slot_cap = max(2, slot_total // seq_count)
    slot_order = jnp.arange(slot_total)
    slot_rank = jnp.sum(
        (owners[:, None] == owners[None, :]) & (slot_order[:, None] > slot_order[None, :]), axis=1
    )
    placed = (owners * slot_cap + slot_rank)[:, None] == jnp.arange(seq_count * slot_cap)[None, :]
    placed_light = placed.astype(jnp.bfloat16)
    request = jnp.sum(jnp.where(placed, wanted[:, None] + 1, 0), axis=0).reshape(
        seq_count, slot_cap
    )
    asked_for = lax.all_to_all(request, "seq", split_axis=0, concat_axis=0, tiled=True).reshape(-1)
    served = ((asked_for - 1)[:, None] == jnp.arange(blk_count)[None, :]).astype(jnp.bfloat16)
    all_keys, all_values = (
        lax.all_gather(keys, "seq", axis=0, tiled=True),
        lax.all_gather(values, "seq", axis=0, tiled=True),
    )
    picked = (
        (owners * blk_count + wanted)[:, None] == jnp.arange(blk_count * seq_count)[None, :]
    ).astype(jnp.bfloat16)
    ref_keys = jnp.dot(
        picked,
        all_keys.reshape(blk_count * seq_count, blk_width),
        preferred_element_type=jnp.float32,
    )
    ref_values = jnp.dot(
        picked,
        all_values.reshape(blk_count * seq_count, blk_width),
        preferred_element_type=jnp.float32,
    )
    ref_keys = ref_keys.astype(jnp.bfloat16).reshape(blk_count, XREF, BLK, key_value_width)
    ref_values = ref_values.astype(jnp.bfloat16).reshape(blk_count, XREF, BLK, key_value_width)
    window_keys = jnp.stack(
        [extended_keys[offset : offset + blk_count] for offset in range(LOOK)], axis=1
    )
    window_values = jnp.stack(
        [extended_values[offset : offset + blk_count] for offset in range(LOOK)], axis=1
    )
    key_sets = jnp.concatenate([window_keys, up_keys, ref_keys], axis=1)
    value_sets = jnp.concatenate([window_values, up_values, ref_values], axis=1)
    positions = jnp.arange(BLK)
    causal = positions[None, :] <= positions[:, None]
    is_last = jnp.arange(LOOK) == LOOK - 1
    padded_sec = jnp.concatenate([jnp.full((behind,), -1, jnp.int32), block_section])
    extended_sec = lax.dynamic_slice_in_dim(padded_sec, first_blk, blk_count + behind)
    window_sec = jnp.stack(
        [extended_sec[offset : offset + blk_count] for offset in range(LOOK)], axis=1
    )
    own_ok = window_sec == my_sec[:, None]
    own_allowed = own_ok[:, None, :, None] & (
        jnp.logical_not(is_last)[None, None, :, None] | causal[None, :, None, :]
    )
    up_allowed = jnp.broadcast_to(
        (ancestors >= 0).reshape(blk_count, ANC)[:, None, :, None], (blk_count, BLK, ANC, BLK)
    )
    ref_allowed = jnp.broadcast_to((xref_valid > 0)[:, None, :, None], (blk_count, BLK, XREF, BLK))
    allowed = jnp.concatenate([own_allowed, up_allowed, ref_allowed], axis=2).reshape(
        blk_count, BLK, key_count * BLK
    )
    query_blocks = queries.reshape(blk_count, BLK, -1)
    attn_blocks = lax.map(run_forward, (query_blocks, key_sets, value_sets, allowed))
    attn = attn_blocks.reshape(tok_local, -1)
    d_full = lax.all_gather(d_proj, "head", axis=1, tiled=True)
    partials = jnp.dot(
        attn,
        lax.all_gather(out_weight, "seq", axis=1, tiled=True),
        preferred_element_type=jnp.float32,
    )
    d_attn = lax.dot_general(
        d_full,
        lax.all_gather(out_weight, "seq", axis=1, tiled=True),
        (((1,), (1,)), ((), ())),
        preferred_element_type=jnp.float32,
    ).astype(jnp.bfloat16)
    projected = lax.psum_scatter(
        partials.astype(jnp.bfloat16), "head", scatter_dimension=1, tiled=True
    )
    grad_queries, key_terms, value_terms = lax.map(
        run_backward,
        (
            query_blocks,
            key_sets,
            value_sets,
            allowed,
            attn_blocks,
            d_attn.reshape(blk_count, BLK, -1),
        ),
    )

    def spread(terms):
        extended = jnp.zeros((blk_count + behind, blk_width), jnp.float32)
        for offset in range(LOOK):
            extended = extended.at[offset : offset + blk_count].add(terms[:, offset])
        return extended

    extended_dk = spread(key_terms)
    extended_dv = spread(value_terms)
    next_dk, next_dv = (
        passed_along(extended_dk[:behind].astype(jnp.bfloat16), "seq", -1).astype(jnp.float32),
        passed_along(extended_dv[:behind].astype(jnp.bfloat16), "seq", -1).astype(jnp.float32),
    )
    own_dk = extended_dk[behind:] + jnp.pad(next_dk, ((blk_count - behind, 0), (0, 0)))
    own_dv = extended_dv[behind:] + jnp.pad(next_dv, ((blk_count - behind, 0), (0, 0)))
    chosen_float = chosen_up.T.astype(jnp.float32)
    section_dk = jnp.dot(
        chosen_float,
        key_terms[:, LOOK : LOOK + ANC].reshape(blk_count * ANC, blk_width),
        precision=lax.Precision.HIGHEST,
    )
    section_dv = jnp.dot(
        chosen_float,
        value_terms[:, LOOK : LOOK + ANC].reshape(blk_count * ANC, blk_width),
        precision=lax.Precision.HIGHEST,
    )
    summed_dk, summed_dv = (
        lax.psum(section_dk.astype(jnp.bfloat16), "seq").astype(jnp.float32),
        lax.psum(section_dv.astype(jnp.bfloat16), "seq").astype(jnp.float32),
    )
    spread_down = (mine / root_counts[:, None]).T
    up_dk = jnp.dot(spread_down, summed_dk, precision=lax.Precision.HIGHEST)
    up_dv = jnp.dot(spread_down, summed_dv, precision=lax.Precision.HIGHEST)
    slot_dk_light = (
        key_terms[:, LOOK + ANC :].reshape(blk_count * XREF, blk_width).astype(jnp.bfloat16)
    )
    slot_dv_light = (
        value_terms[:, LOOK + ANC :].reshape(blk_count * XREF, blk_width).astype(jnp.bfloat16)
    )
    placed_back = placed_light.T
    slot_dk = (
        jnp.dot(placed_back, slot_dk_light, preferred_element_type=jnp.float32)
        .astype(jnp.bfloat16)
        .reshape(seq_count, slot_cap, blk_width)
    )
    slot_dv = (
        jnp.dot(placed_back, slot_dv_light, preferred_element_type=jnp.float32)
        .astype(jnp.bfloat16)
        .reshape(seq_count, slot_cap, blk_width)
    )
    back_dk, back_dv = (
        lax.all_to_all(slot_dk, "seq", split_axis=0, concat_axis=0, tiled=True),
        lax.all_to_all(slot_dv, "seq", split_axis=0, concat_axis=0, tiled=True),
    )
    served_back = served.T
    ref_dk = jnp.dot(
        served_back,
        back_dk.reshape(seq_count * slot_cap, blk_width),
        preferred_element_type=jnp.float32,
    )
    ref_dv = jnp.dot(
        served_back,
        back_dv.reshape(seq_count * slot_cap, blk_width),
        preferred_element_type=jnp.float32,
    )
    d_keys = (own_dk + up_dk + ref_dk).astype(jnp.bfloat16).reshape(tok_local, key_value_width)
    d_values = (own_dv + up_dv + ref_dv).astype(jnp.bfloat16).reshape(tok_local, key_value_width)
    return (projected, grad_queries.reshape(tok_local, -1), d_keys, d_values)


def solution(mesh):
    placed = (
        P("seq", "head"),
        P("seq", "head"),
        P("seq", "head"),
        P("head", "seq"),
        P("seq", "head"),
        P(),
        P(),
        P("seq", None),
        P("seq", None),
        P("seq", None),
    )
    return jax.shard_map(
        on_device,
        mesh=mesh,
        in_specs=placed,
        out_specs=(P("seq", "head"), P("seq", "head"), P("seq", "head"), P("seq", "head")),
        check_vma=False,
    )
```

profile of v0, /device:TPU:0, one launch (start us, length us, event | category | flops | bytes accessed | tf_op | source)
XLA Modules:
  0.0 916.1 jit_solution(16726008169949510569)
XLA Ops:
  15.9 5.5 collective-permute-start
  25.4 4.8 all-to-all-start
  45.3 45.7 %all-reduce.12.cloned.1.call-done = (bf16[4,32768]{1,0:T(4,128)(2,1)}, bf16[4,32768]{1,0:T(4,128)(2,1)}) async-done(((bf16[4,32768]{1,0:T(4,128)(2,1)}, bf16[4,32768]{1,0:T(4,128)(2,1)}), (bf16[4,32768]{1,0:T(4,128)(2,1)}, bf16[4,32768]{1,0:T(4,128)(2,1)})) %all-reduce.12.cloned.1.call-update) | async-done | bytes 524304 | tf_op jit(solution)/shard_map/psum | solution.py:153
  95.5 45.9 %all-gather.5.cloned.1.call-done = bf16[4096,256]{1,0:T(8,128)(2,1)} async-done(((bf16[512,256]{1,0:T(8,128)(2,1)}), bf16[4096,256]{1,0:T(8,128)(2,1)}) %all-gather.5.cloned.1.call-update) | async-done | bytes 2097168 | tf_op jit(solution)/shard_map/all_gather | solution.py:185
  146.0 45.1 %all-gather.7.cloned.1.call-done = bf16[4096,256]{1,0:T(8,128)(2,1)} async-done(((bf16[512,256]{1,0:T(8,128)(2,1)}), bf16[4096,256]{1,0:T(8,128)(2,1)}) %all-gather.7.cloned.1.call-update) | async-done | bytes 2097168 | tf_op jit(solution)/shard_map/all_gather | solution.py:184
  191.2 4.3 reshape.487
  202.0 95.5 %while.32 = (s32[]{:T(128)}, bf16[4,128,1280]{1,2,0:T(8,128)(2,1)}, bf16[4,18,128,256]{3,2,1,0:T(8,128)(2,1)}, pred[4,128,2304]{2,1,0:T(8,128)(4,1)}, bf16[4,128...) while((s32[]{:T(128)}, bf16[4,128,1280]{1,2,0:T(8,128)(2,1)}, ...), condition=%wide.region_7.8_spmd, body=%wide.region_4.0_spmd.sunk | while | flops 1530759424 | bytes 38250596 | solution.py:230
  207.8 10.7 %fusion.123 = (f32[2,128,5]{1,2,0:T(8,128)S(1)}, f32[2,128,5,2304]{3,1,2,0:T(8,128)}) fusion(pred[128,2304]{1,0:T(8,128)(4,1)} %dynamic-slice_bitcast_fusion.5, bf16[128,2,5,128]{0,3,2,1:T(8,128)(2,1)} %bitcast.225, bf16[2304,2,128,1]{2,1,0,3:T(2,128)(2,1)S(1)} %bitcast.217), kind=kOutput, calls=%fused_computation.159.clone.1 | convolution fusion | flops 769722624 | bytes 13603840 | tf_op jit(solution)/shard_map/while/body/eval_jaxpr/sub | solution.py:34
  218.8 6.4 fusion.124
  231.6 10.7 %fusion.123 = (f32[2,128,5]{1,2,0:T(8,128)S(1)}, f32[2,128,5,2304]{3,1,2,0:T(8,128)}) fusion(pred[128,2304]{1,0:T(8,128)(4,1)} %dynamic-slice_bitcast_fusion.5, bf16[128,2,5,128]{0,3,2,1:T(8,128)(2,1)} %bitcast.225, bf16[2304,2,128,1]{2,1,0,3:T(2,128)(2,1)S(1)} %bitcast.217), kind=kOutput, calls=%fused_computation.159.clone.1 | convolution fusion | flops 769722624 | bytes 13603840 | tf_op jit(solution)/shard_map/while/body/eval_jaxpr/sub | solution.py:34
  242.5 6.5 fusion.124
  255.3 10.9 %fusion.123 = (f32[2,128,5]{1,2,0:T(8,128)S(1)}, f32[2,128,5,2304]{3,1,2,0:T(8,128)}) fusion(pred[128,2304]{1,0:T(8,128)(4,1)} %dynamic-slice_bitcast_fusion.5, bf16[128,2,5,128]{0,3,2,1:T(8,128)(2,1)} %bitcast.225, bf16[2304,2,128,1]{2,1,0,3:T(2,128)(2,1)S(1)} %bitcast.217), kind=kOutput, calls=%fused_computation.159.clone.1 | convolution fusion | flops 769722624 | bytes 13603840 | tf_op jit(solution)/shard_map/while/body/eval_jaxpr/sub | solution.py:34
  266.5 6.5 fusion.124
  279.3 10.7 %fusion.123 = (f32[2,128,5]{1,2,0:T(8,128)S(1)}, f32[2,128,5,2304]{3,1,2,0:T(8,128)}) fusion(pred[128,2304]{1,0:T(8,128)(4,1)} %dynamic-slice_bitcast_fusion.5, bf16[128,2,5,128]{0,3,2,1:T(8,128)(2,1)} %bitcast.225, bf16[2304,2,128,1]{2,1,0,3:T(2,128)(2,1)S(1)} %bitcast.217), kind=kOutput, calls=%fused_computation.159.clone.1 | convolution fusion | flops 769722624 | bytes 13603840 | tf_op jit(solution)/shard_map/while/body/eval_jaxpr/sub | solution.py:34
  290.2 6.5 fusion.124
  299.9 20.7 %all-gather.9.cloned.1.call-done = bf16[1280,2560]{0,1:T(8,128)(2,1)} async-done(((bf16[1280,320]{0,1:T(8,128)(2,1)}), bf16[1280,2560]{0,1:T(8,128)(2,1)}) %all-gather.9.cloned.1.call-update) | async-done | bytes 6553616 | tf_op jit(solution)/shard_map/all_gather | solution.py:235
  320.6 8.3 convolution_convert_fusion.10
  328.9 252.5 %while.33 = (s32[]{:T(128)}, bf16[4,128,1280]{2,1,0:T(8,128)(2,1)}, f32[4,18,32768]{2,1,0:T(8,128)}, f32[4,18,32768]{2,1,0:T(8,128)}, bf16[4,18,128,256]{3,2,1,0...) while((s32[]{:T(128)}, bf16[4,128,1280]{2,1,0:T(8,128)(2,1)}, ...), condition=%wide.region_12.13_spmd, body=%wide.region_9.12_spmd.sunk | while | flops 3811083264 | bytes 134538416 | solution.py:247
  336.8 8.3 fusion.136
  347.5 7.6 multiply_convert_fusion.2
  360.4 5.2 fusion.137
  365.6 3.2 copy.208
  368.8 3.6 broadcast_in_dim.169
  372.4 5.2 convolution_bitcast_fusion.2
  377.6 4.9 copy.209
  382.6 4.8 broadcast_in_dim.170
  387.3 4.9 constant_dynamic-update-slice_fusion.25
  399.7 8.3 fusion.136
  410.5 7.6 multiply_convert_fusion.2
  423.3 5.2 fusion.137
  431.7 3.6 broadcast_in_dim.169
  435.3 5.2 convolution_bitcast_fusion.2
  440.6 4.9 copy.209
  445.5 4.8 broadcast_in_dim.170
  450.2 4.9 constant_dynamic-update-slice_fusion.25
  462.6 8.3 fusion.136
  473.4 7.6 multiply_convert_fusion.2
  486.3 5.2 fusion.137
  494.7 3.6 broadcast_in_dim.169
  498.3 5.2 convolution_bitcast_fusion.2
  503.5 4.9 copy.209
  508.4 4.8 broadcast_in_dim.170
  513.2 5.1 constant_dynamic-update-slice_fusion.25
  525.7 8.3 fusion.136
  536.5 7.6 multiply_convert_fusion.2
  549.4 5.2 fusion.137
  557.8 3.6 broadcast_in_dim.169
  561.4 5.2 convolution_bitcast_fusion.2
  566.6 4.9 copy.209
  571.5 4.8 broadcast_in_dim.170
  576.3 4.9 constant_dynamic-update-slice_fusion.25
  584.0 14.2 %copy.134 = f32[4,18,32768]{2,0,1:T(4,128)} copy(f32[4,18,32768]{2,1,0:T(8,128)} %get-tuple-element.188) | data formatting | bytes 18874368 | tf_op jit(solution)/shard_map/while | solution.py:247
  598.2 7.2 slice.345
  608.1 14.5 %copy.139 = f32[4,18,32768]{2,0,1:T(4,128)} copy(f32[4,18,32768]{2,1,0:T(8,128)} %get-tuple-element.189) | data formatting | bytes 18874368 | tf_op jit(solution)/shard_map/while | solution.py:247
  622.6 7.5 slice.344
  630.1 7.7 convolution_convert_fusion.9
  637.8 4.5 copy.170
  661.2 4.0 reshape.496
  665.2 5.5 all-to-all-start.1
  679.9 4.1 reshape.503
  686.9 84.2 %all-to-all-done.1 = bf16[8,6,32768]{2,1,0:T(8,128)(2,1)} async-done(((bf16[8,6,32768]{2,1,0:T(8,128)(2,1)}), bf16[8,6,32768]{2,1,0:T(8,128)(2,1)}, u32[]{:S(2)}, u32[]{:S(2)}) %all-to-all-start.1) | async-done | bytes 3145760 | tf_op jit(solution)/shard_map/all_to_all | solution.py:309
  771.2 4.6 all-to-all-start.2
  780.9 76.7 %all-reduce.10.cloned.1.call-done = (bf16[4,32768]{1,0:T(4,128)(2,1)}, bf16[4,32768]{1,0:T(4,128)(2,1)}) async-done(((bf16[4,32768]{1,0:T(4,128)(2,1)}, bf16[4,32768]{1,0:T(4,128)(2,1)}), (bf16[4,32768]{1,0:T(4,128)(2,1)}, bf16[4,32768]{1,0:T(4,128)(2,1)})) %all-reduce.10.cloned.1.call-update) | async-done | bytes 524304 | tf_op jit(solution)/shard_map/psum | solution.py:285
  862.6 31.7 %reduce-scatter.4.cloned.1.call-done = bf16[640,512]{1,0:T(8,128)(2,1)} async-done(((bf16[2560,512]{1,0:T(8,128)(2,1)}), bf16[640,512]{1,0:T(8,128)(2,1)}) %reduce-scatter.4.cloned.1.call-update) | async-done | bytes 655376
  (263 shorter events, 203.1 us)
Async XLA Ops:
  7.2 83.8 %all-reduce.12.cloned.1.call-start = ((), (), s32[]{:S(2)}) async-start(), calls=%async_computation.10 | async-start | bytes 1048576 | tf_op jit(solution)/shard_map/psum | solution.py:153
  9.1 3.9 copy-start.17
  9.9 21.5 %copy-start.15 = (s32[4]{0:T(128)}, s32[4]{0:T(128)S(1)}, u32[]{:S(2)}) copy-start(s32[4]{0:T(128)S(1)} %dynamic_slice.39) | copy-start | bytes 52
  11.0 4.1 copy-start.4
  11.0 10.4 %copy-start.5 = (bf16[512,256]{1,0:T(8,128)(2,1)S(1)}, bf16[512,256]{1,0:T(8,128)(2,1)}, u32[]{:S(2)}) copy-start(bf16[512,256]{1,0:T(8,128)(2,1)} %param.31) | copy-start | bytes 786436
  11.1 13.2 %copy-start.11 = (s32[4,12]{1,0:T(4,128)S(1)}, s32[4,12]{1,0:T(4,128)}, u32[]{:S(2)}) copy-start(s32[4,12]{1,0:T(4,128)} %param.38) | copy-start | bytes 580
  11.1 13.3 %copy-start.20 = (s32[48,1]{0,1:T(1,128)S(1)}, s32[48,1]{0,1:T(1,128)}, u32[]{:S(2)}) copy-start(s32[48,1]{0,1:T(1,128)} %param.37) | copy-start | bytes 580
  12.1 18.7 %copy-start.21 = (s32[32]{0:T(128)S(1)}, s32[32]{0:T(128)}, u32[]{:S(2)}) copy-start(s32[32]{0:T(128)} %param.35) | copy-start | bytes 388
  12.1 18.9 %copy-start.22 = (s32[4]{0:T(128)S(1)}, s32[4]{0:T(128)}, u32[]{:S(2)}) copy-start(s32[4]{0:T(128)} %param.36) | copy-start | bytes 52
  12.1 19.0 %copy-start.19 = (s32[4,12]{1,0:T(4,128)S(1)}, s32[4,12]{1,0:T(4,128)}, u32[]{:S(2)}) copy-start(s32[4,12]{1,0:T(4,128)} %param.39) | copy-start | bytes 580
  13.1 128.3 %all-gather.5.cloned.1.call-start = ((), (), s32[]{:S(2)}) async-start(), calls=%async_computation.4 | async-start | bytes 2359296 | tf_op jit(solution)/shard_map/all_gather | solution.py:185
  13.8 177.3 %all-gather.7.cloned.1.call-start = ((), (), s32[]{:S(2)}) async-start(), calls=%async_computation.5 | async-start | bytes 2359296 | tf_op jit(solution)/shard_map/all_gather | solution.py:184
  14.6 285.3 %all-gather.11.cloned.1.call-start = ((), (), s32[]{:S(2)}) async-start(), calls=%async_computation.7 | async-start | bytes 3276800 | tf_op jit(solution)/shard_map/all_gather | solution.py:232
  15.9 22.4 %collective-permute-start = (bf16[384,256]{1,0:T(8,128)(2,1)}, bf16[384,256]{1,0:T(8,128)(2,1)}, u32[]{:S(2)}, u32[]{:S(2)}) collective-permute-start(bf16[384,256]{1,0:T(8,128)(2,1)} %slice.240), channel_id=1, source_target_pairs={{0,4},{4,8},{8,12},{12,16},{16,20},{20,24},{24,28},{1,5},{5,9},{9,... | collective-permute-start | bytes 589832 | tf_op jit(solution)/shard_map/ppermute | solution.py:17
  21.4 18.6 %collective-permute-start.1 = (bf16[384,256]{1,0:T(8,128)(2,1)S(1)}, bf16[384,256]{1,0:T(8,128)(2,1)S(1)}, u32[]{:S(2)}, u32[]{:S(2)}) collective-permute-start(bf16[384,256]{1,0:T(8,128)(2,1)S(1)} %slice.248), channel_id=1, source_target_pairs={{0,4},{4,8},{8,12},{12,16},{16,20},{20,24},{24,28},{1,5},{5,9},{9,... | collective-permute-start | bytes 589832 | tf_op jit(solution)/shard_map/ppermute | solution.py:17
  24.6 0.8 copy-start.12
  25.4 12.2 %all-to-all-start = ((s32[8,1,6]{2,1,0:T(1,128)}), s32[8,1,6]{2,1,0:T(1,128)S(1)}, u32[]{:S(2)}, u32[]{:S(2)}) async-start(s32[8,1,6]{2,1,0:T(1,128)} %bitcast.52), calls=%async_computation | async-start | bytes 8192 | tf_op jit(solution)/shard_map/all_to_all | solution.py:181
  30.2 290.4 %all-gather.9.cloned.1.call-start = ((), (), s32[]{:S(2)}) async-start(), calls=%async_computation.6 | async-start | bytes 7372800 | tf_op jit(solution)/shard_map/all_gather | solution.py:235
  32.5 59.9 %copy-start.9 = (s32[8]{0:T(128)}, s32[8]{0:T(128)S(1)}, u32[]{:S(2)}) copy-start(s32[8]{0:T(128)S(1)} %eq.130) | copy-start | bytes 100
  355.1 2.5 copy-start
  418.1 2.5 copy-start
  481.0 2.5 copy-start
  544.1 2.5 copy-start
  622.6 7.5 copy-start.8
  637.8 5.2 copy-start.10
  653.5 1.0 copy-start.3
  653.5 4.9 copy-start.13
  654.4 244.9 %collective-permute-start.2 = (bf16[3,32768]{1,0:T(4,128)(2,1)S(1)}, bf16[3,32768]{1,0:T(4,128)(2,1)}, u32[]{:S(2)}, u32[]{:S(2)}) collective-permute-start(bf16[3,32768]{1,0:T(4,128)(2,1)S(1)} %slice.347), channel_id=1, source_target_pairs={{4,0},{8,4},{12,8},{16,12},{20,16},{24,20},{28,24},{5,1},{9,5},{13... | collective-permute-start | bytes 589832 | tf_op jit(solution)/shard_map/ppermute | solution.py:17
  665.2 106.0 %all-to-all-start.1 = ((bf16[8,6,32768]{2,1,0:T(8,128)(2,1)}), bf16[8,6,32768]{2,1,0:T(8,128)(2,1)}, u32[]{:S(2)}, u32[]{:S(2)}) async-start(bf16[8,6,32768]{2,1,0:T(8,128)(2,1)} %reshape.496), calls=%async_computation.1 | async-start | bytes 8388608 | tf_op jit(solution)/shard_map/all_to_all | solution.py:309
  670.7 186.8 %all-reduce.10.cloned.1.call-start = ((), (), s32[]{:S(2)}) async-start(), calls=%async_computation.9 | async-start | bytes 1048576 | tf_op jit(solution)/shard_map/psum | solution.py:285
  671.3 223.0 %reduce-scatter.4.cloned.1.call-start = ((), (), s32[]{:S(2)}) async-start(), calls=%async_computation.8 | async-start | bytes 3276800
  672.4 0.8 copy-start.6
  679.9 4.1 copy-start.7
  679.9 5.3 copy-start.1
  686.9 170.6 %copy-start.16 = (s32[4]{0:T(128)S(1)}, s32[4]{0:T(128)}, u32[]{:S(2)}) copy-start(s32[4]{0:T(128)} %copy-done.15) | copy-start | bytes 52
  686.9 170.6 %copy-start.18 = (f32[4]{0:T(128)S(1)}, f32[4]{0:T(128)}, u32[]{:S(2)}) copy-start(f32[4]{0:T(128)} %copy-done.17) | copy-start | bytes 52
  771.2 131.5 %all-to-all-start.2 = ((bf16[8,6,32768]{2,1,0:T(8,128)(2,1)}), bf16[8,6,32768]{2,1,0:T(8,128)(2,1)}, u32[]{:S(2)}, u32[]{:S(2)}) async-start(bf16[8,6,32768]{2,1,0:T(8,128)(2,1)} %reshape.503), calls=%async_computation.2 | async-start | bytes 8388608 | tf_op jit(solution)/shard_map/all_to_all | solution.py:310
  778.7 115.7 %copy-start.2 = (f32[7,32768]{1,0:T(8,128)}, f32[7,32768]{1,0:T(8,128)S(1)}, u32[]{:S(2)}) copy-start(f32[7,32768]{1,0:T(8,128)S(1)} %scatter-add.29) | copy-start | bytes 2752516
  779.6 125.9 %collective-permute-start.3 = (bf16[3,32768]{1,0:T(4,128)(2,1)}, bf16[3,32768]{1,0:T(4,128)(2,1)}, u32[]{:S(2)}, u32[]{:S(2)}) collective-permute-start(bf16[3,32768]{1,0:T(4,128)(2,1)} %slice.346), channel_id=1, source_target_pairs={{4,0},{8,4},{12,8},{16,12},{20,16},{24,20},{28,24},{5,1},{9,5},{13... | collective-permute-start | bytes 589832 | tf_op jit(solution)/shard_map/ppermute | solution.py:17
  894.3 5.0 copy-start.14
Sparse Core Ops, SparseCore 0:
  13.2 77.6 all-reduce.11
  93.1 48.2 all-gather.4
  143.5 47.6 all-gather.6
  192.6 24.0 all-gather.10
  218.7 101.8 all-gather.8
  675.3 182.2 all-reduce.9
  860.1 34.2 reduce-scatter.3
where the time goes:
time: 927 us; the launch traced here: 916 us
  waiting for transfers between devices  353 us (38%)
  local copies, waits for them, and re-layouts  290 us (31%)
  matrix products  224 us (24%)
  starting transfers between devices  26.1 us (3%)
  between operations  15.2 us (2%)
    dot_general x20, matrix products, product(): return jnp.einsum(form, left, right, preferred_element_type=jnp.float32)  105 us
    all_to_all x1, waiting for transfers between devices, on_device(): lax.all_to_all(slot_dk, 'seq', split_axis=0, concat_axis=0, tiled=True)  84.2 us
    psum x1, waiting for transfers between devices, on_device(): lax.psum(section_dk.astype(jnp.bfloat16), 'seq').astype(jnp.float32)  76.7 us
    sub x8, matrix products, softmax_weights(): exponent = jnp.where(allowed, jnp.exp(masked - row_max), 0.0)  75.9 us
    all_gather x1, waiting for transfers between devices, on_device(): lax.all_gather(values, 'seq', axis=0, tiled=True)  45.9 us
    psum x1, waiting for transfers between devices, on_device(): lax.psum(part_values.astype(jnp.bfloat16), 'seq').astype(jnp.float32)  45.7 us
    all_gather x1, waiting for transfers between devices, on_device(): lax.all_gather(keys, 'seq', axis=0, tiled=True)  45.1 us
    dynamic_slice x32, local copies, waits for them, and re-layouts, on_device(): lax.map(run_forward, (query_blocks, key_sets, value_sets, allowed))  37.7 us
  transfers between devices with their start and end apart: 14, of which 7 were waited for; matrix products, arithmetic and copies ran while one was open for 19% of the time, Pallas kernels for 0%

commit v1 on v0

--- a/solution.py
+++ b/solution.py
@@ -101,6 +101,11 @@
     xref_block,
     xref_valid,
 ):
+
+    def sheet_render(view):
+        back = jnp.sum(lax.all_gather(view, "seq"), axis=0)
+        return back
+
     seq_count = lax.axis_size("seq")
     seq_rank = lax.axis_index("seq")
     tok_local = queries.shape[0]
@@ -282,7 +287,7 @@
         precision=lax.Precision.HIGHEST,
     )
     summed_dk, summed_dv = (
-        lax.psum(section_dk.astype(jnp.bfloat16), "seq").astype(jnp.float32),
+        sheet_render(section_dk.astype(jnp.bfloat16)).astype(jnp.float32),
         lax.psum(section_dv.astype(jnp.bfloat16), "seq").astype(jnp.float32),
     )
     spread_down = (mine / root_counts[:, None]).T

time: 927 us -> 964 us (1.040)
  waiting for transfers between devices: 353 us -> 384 us
    all_gather x0 -> x1, waiting for transfers between devices: none -> 89.9 us  [sheet_render(): back = jnp.sum(lax.all_gather(view, 'seq'), axis=0)]
    psum x1, waiting for transfers between devices: 76.7 us -> 22.9 us  [on_device(): lax.psum(section_dv.astype(jnp.bfloat16), 'seq').astype(jnp.float32)]
    unnamed x8 -> x9, waiting for transfers between devices: 34.7 us -> 34.7 us
  transfers between devices with their start and end apart: 14 -> 15, of which waited for: 7 -> 8; matrix products, arithmetic and copies ran while one was open for 19% -> 19% of each run, Pallas kernels for 0% -> 0%
where the time goes in v1:
time: 964 us; the launch traced here: 954 us
  waiting for transfers between devices  384 us (40%)
  local copies, waits for them, and re-layouts  294 us (30%)
  matrix products  224 us (23%)
  starting transfers between devices  26.3 us (3%)
  between operations  15.2 us (2%)
  other arithmetic  9.68 us (1%)
    dot_general x20, matrix products, product(): return jnp.einsum(form, left, right, preferred_element_type=jnp.float32)  105 us
    all_gather x1, waiting for transfers between devices, sheet_render(): back = jnp.sum(lax.all_gather(view, 'seq'), axis=0)  89.9 us
    all_to_all x1, waiting for transfers between devices, on_device(): lax.all_to_all(slot_dk, 'seq', split_axis=0, concat_axis=0, tiled=True)  78.4 us
    sub x8, matrix products, softmax_weights(): exponent = jnp.where(allowed, jnp.exp(masked - row_max), 0.0)  76 us
    all_gather x1, waiting for transfers between devices, on_device(): lax.all_gather(values, 'seq', axis=0, tiled=True)  45.9 us
    psum x1, waiting for transfers between devices, on_device(): lax.psum(part_values.astype(jnp.bfloat16), 'seq').astype(jnp.float32)  45.8 us
    all_gather x1, waiting for transfers between devices, on_device(): lax.all_gather(keys, 'seq', axis=0, tiled=True)  45.1 us
    dynamic_slice x32, local copies, waits for them, and re-layouts, on_device(): lax.map(run_forward, (query_blocks, key_sets, value_sets, allowed))  37.7 us
  transfers between devices with their start and end apart: 15, of which 8 were waited for; matrix products, arithmetic and copies ran while one was open for 19% of the time, Pallas kernels for 0%

profile of v1, /device:TPU:0, one launch (start us, length us, event | category | flops | bytes accessed | tf_op | source)
XLA Modules:
  0.0 953.7 jit_solution(747044220377853183)
XLA Ops:
  15.9 5.5 collective-permute-start
  25.4 4.8 all-to-all-start
  45.1 45.8 %all-reduce.11.cloned.1.call-done = (bf16[4,32768]{1,0:T(4,128)(2,1)}, bf16[4,32768]{1,0:T(4,128)(2,1)}) async-done(((bf16[4,32768]{1,0:T(4,128)(2,1)}, bf16[4,32768]{1,0:T(4,128)(2,1)}), (bf16[4,32768]{1,0:T(4,128)(2,1)}, bf16[4,32768]{1,0:T(4,128)(2,1)})) %all-reduce.11.cloned.1.call-update) | async-done | bytes 524304 | tf_op jit(solution)/shard_map/psum | solution.py:158
  95.5 45.9 %all-gather.8.cloned.1.call-done = bf16[4096,256]{1,0:T(8,128)(2,1)} async-done(((bf16[512,256]{1,0:T(8,128)(2,1)}), bf16[4096,256]{1,0:T(8,128)(2,1)}) %all-gather.8.cloned.1.call-update) | async-done | bytes 2097168 | tf_op jit(solution)/shard_map/all_gather | solution.py:190
  146.0 45.1 %all-gather.10.cloned.1.call-done = bf16[4096,256]{1,0:T(8,128)(2,1)} async-done(((bf16[512,256]{1,0:T(8,128)(2,1)}), bf16[4096,256]{1,0:T(8,128)(2,1)}) %all-gather.10.cloned.1.call-update) | async-done | bytes 2097168 | tf_op jit(solution)/shard_map/all_gather | solution.py:189
  191.2 4.3 reshape.487
  202.0 95.4 %while.32 = (s32[]{:T(128)}, bf16[4,128,1280]{1,2,0:T(8,128)(2,1)}, bf16[4,18,128,256]{3,2,1,0:T(8,128)(2,1)}, pred[4,128,2304]{2,1,0:T(8,128)(4,1)}, bf16[4,128...) while((s32[]{:T(128)}, bf16[4,128,1280]{1,2,0:T(8,128)(2,1)}, ...), condition=%wide.region_7.8_spmd, body=%wide.region_4.0_spmd.sunk | while | flops 1530759424 | bytes 38250596 | solution.py:235
  207.8 10.7 %fusion.124 = (f32[2,128,5]{1,2,0:T(8,128)S(1)}, f32[2,128,5,2304]{3,1,2,0:T(8,128)}) fusion(pred[128,2304]{1,0:T(8,128)(4,1)} %dynamic-slice_bitcast_fusion.5, bf16[128,2,5,128]{0,3,2,1:T(8,128)(2,1)} %bitcast.227, bf16[2304,2,128,1]{2,1,0,3:T(2,128)(2,1)S(1)} %bitcast.219), kind=kOutput, calls=%fused_computation.160.clone.1 | convolution fusion | flops 769722624 | bytes 13603840 | tf_op jit(solution)/shard_map/while/body/eval_jaxpr/sub | solution.py:34
  218.7 6.4 fusion.125
  231.5 10.7 %fusion.124 = (f32[2,128,5]{1,2,0:T(8,128)S(1)}, f32[2,128,5,2304]{3,1,2,0:T(8,128)}) fusion(pred[128,2304]{1,0:T(8,128)(4,1)} %dynamic-slice_bitcast_fusion.5, bf16[128,2,5,128]{0,3,2,1:T(8,128)(2,1)} %bitcast.227, bf16[2304,2,128,1]{2,1,0,3:T(2,128)(2,1)S(1)} %bitcast.219), kind=kOutput, calls=%fused_computation.160.clone.1 | convolution fusion | flops 769722624 | bytes 13603840 | tf_op jit(solution)/shard_map/while/body/eval_jaxpr/sub | solution.py:34
  242.5 6.5 fusion.125
  255.2 10.9 %fusion.124 = (f32[2,128,5]{1,2,0:T(8,128)S(1)}, f32[2,128,5,2304]{3,1,2,0:T(8,128)}) fusion(pred[128,2304]{1,0:T(8,128)(4,1)} %dynamic-slice_bitcast_fusion.5, bf16[128,2,5,128]{0,3,2,1:T(8,128)(2,1)} %bitcast.227, bf16[2304,2,128,1]{2,1,0,3:T(2,128)(2,1)S(1)} %bitcast.219), kind=kOutput, calls=%fused_computation.160.clone.1 | convolution fusion | flops 769722624 | bytes 13603840 | tf_op jit(solution)/shard_map/while/body/eval_jaxpr/sub | solution.py:34
  266.5 6.5 fusion.125
  279.2 10.7 %fusion.124 = (f32[2,128,5]{1,2,0:T(8,128)S(1)}, f32[2,128,5,2304]{3,1,2,0:T(8,128)}) fusion(pred[128,2304]{1,0:T(8,128)(4,1)} %dynamic-slice_bitcast_fusion.5, bf16[128,2,5,128]{0,3,2,1:T(8,128)(2,1)} %bitcast.227, bf16[2304,2,128,1]{2,1,0,3:T(2,128)(2,1)S(1)} %bitcast.219), kind=kOutput, calls=%fused_computation.160.clone.1 | convolution fusion | flops 769722624 | bytes 13603840 | tf_op jit(solution)/shard_map/while/body/eval_jaxpr/sub | solution.py:34
  290.2 6.5 fusion.125
  299.8 20.8 %all-gather.12.cloned.1.call-done = bf16[1280,2560]{0,1:T(8,128)(2,1)} async-done(((bf16[1280,320]{0,1:T(8,128)(2,1)}), bf16[1280,2560]{0,1:T(8,128)(2,1)}) %all-gather.12.cloned.1.call-update) | async-done | bytes 6553616 | tf_op jit(solution)/shard_map/all_gather | solution.py:240
  320.6 8.3 convolution_convert_fusion.10
  328.9 252.4 %while.33 = (s32[]{:T(128)}, bf16[4,128,1280]{2,1,0:T(8,128)(2,1)}, f32[4,18,32768]{2,1,0:T(8,128)}, f32[4,18,32768]{2,1,0:T(8,128)}, bf16[4,18,128,256]{3,2,1,0...) while((s32[]{:T(128)}, bf16[4,128,1280]{2,1,0:T(8,128)(2,1)}, ...), condition=%wide.region_12.13_spmd, body=%wide.region_9.12_spmd.sunk | while | flops 3811083264 | bytes 134538416 | solution.py:252
  336.7 8.3 fusion.137
  347.5 7.6 multiply_convert_fusion.2
  360.4 5.2 fusion.138
  368.8 3.6 broadcast_in_dim.169
  372.4 5.2 convolution_bitcast_fusion.2
  377.6 4.9 copy.210
  382.5 4.8 broadcast_in_dim.170
  387.3 4.9 constant_dynamic-update-slice_fusion.25
  399.6 8.3 fusion.137
  410.4 7.6 multiply_convert_fusion.2
  423.3 5.2 fusion.138
  431.6 3.6 broadcast_in_dim.169
  435.3 5.2 convolution_bitcast_fusion.2
  440.5 4.9 copy.210
  445.4 4.8 broadcast_in_dim.170
  450.2 4.9 constant_dynamic-update-slice_fusion.25
  462.5 8.3 fusion.137
  473.3 7.6 multiply_convert_fusion.2
  486.2 5.2 fusion.138
  494.6 3.6 broadcast_in_dim.169
  498.2 5.2 convolution_bitcast_fusion.2
  503.4 4.9 copy.210
  508.3 4.8 broadcast_in_dim.170
  513.1 5.1 constant_dynamic-update-slice_fusion.25
  525.6 8.3 fusion.137
  536.4 7.6 multiply_convert_fusion.2
  549.3 5.2 fusion.138
  557.7 3.6 broadcast_in_dim.169
  561.3 5.2 convolution_bitcast_fusion.2
  566.5 4.9 copy.210
  571.4 4.8 broadcast_in_dim.170
  576.2 4.9 constant_dynamic-update-slice_fusion.25
  583.9 14.2 %copy.134 = f32[4,18,32768]{2,0,1:T(4,128)} copy(f32[4,18,32768]{2,1,0:T(8,128)} %get-tuple-element.188) | data formatting | bytes 18874368 | tf_op jit(solution)/shard_map/while | solution.py:252
  598.1 7.2 slice.345
  609.0 14.5 %copy.139 = f32[4,18,32768]{2,0,1:T(4,128)} copy(f32[4,18,32768]{2,1,0:T(8,128)} %get-tuple-element.189) | data formatting | bytes 18874368 | tf_op jit(solution)/shard_map/while | solution.py:252
  623.5 7.5 slice.344
  630.9 7.8 convolution_convert_fusion.9
  638.7 4.4 copy.170
  665.2 4.0 reshape.496
  669.2 5.6 all-to-all-start.1
  684.9 4.2 reshape.503
  692.1 78.4 %all-to-all-done.1 = bf16[8,6,32768]{2,1,0:T(8,128)(2,1)} async-done(((bf16[8,6,32768]{2,1,0:T(8,128)(2,1)}), bf16[8,6,32768]{2,1,0:T(8,128)(2,1)}, u32[]{:S(2)}, u32[]{:S(2)}) %all-to-all-start.1) | async-done | bytes 3145760 | tf_op jit(solution)/shard_map/all_to_all | solution.py:314
  770.5 4.5 all-to-all-start.2
  780.2 22.9 %all-reduce.9.cloned.1.call-done = bf16[4,32768]{1,0:T(4,128)(2,1)} async-done(((bf16[4,32768]{1,0:T(4,128)(2,1)}), bf16[4,32768]{1,0:T(4,128)(2,1)}) %all-reduce.9.cloned.1.call-update) | async-done | bytes 262160 | tf_op jit(solution)/shard_map/psum | solution.py:291
  805.7 89.9 %all-gather.16.cloned.1.call-done = bf16[8,4,32768]{2,1,0:T(4,128)(2,1)} async-done(((bf16[1,4,32768]{2,1,0:T(4,128)(2,1)}), bf16[8,4,32768]{2,1,0:T(4,128)(2,1)}) %all-gather.16.cloned.1.call-update) | async-done | bytes 2097168 | tf_op jit(solution)/shard_map/all_gather | solution.py:106
  899.7 32.2 %reduce-scatter.4.cloned.1.call-done = bf16[640,512]{1,0:T(8,128)(2,1)} async-done(((bf16[2560,512]{1,0:T(8,128)(2,1)}), bf16[640,512]{1,0:T(8,128)(2,1)}) %reduce-scatter.4.cloned.1.call-update) | async-done | bytes 655376
  (269 shorter events, 212.6 us)
Async XLA Ops:
  7.2 83.8 %all-reduce.11.cloned.1.call-start = ((), (), s32[]{:S(2)}) async-start(), calls=%async_computation.11 | async-start | bytes 1048576 | tf_op jit(solution)/shard_map/psum | solution.py:158
  9.1 3.9 copy-start.18
  9.9 21.5 %copy-start.16 = (s32[4]{0:T(128)}, s32[4]{0:T(128)S(1)}, u32[]{:S(2)}) copy-start(s32[4]{0:T(128)S(1)} %dynamic_slice.39) | copy-start | bytes 52
  11.0 4.1 copy-start.4
  11.0 10.4 %copy-start.5 = (bf16[512,256]{1,0:T(8,128)(2,1)S(1)}, bf16[512,256]{1,0:T(8,128)(2,1)}, u32[]{:S(2)}) copy-start(bf16[512,256]{1,0:T(8,128)(2,1)} %param.31) | copy-start | bytes 786436
  11.1 13.2 %copy-start.12 = (s32[4,12]{1,0:T(4,128)S(1)}, s32[4,12]{1,0:T(4,128)}, u32[]{:S(2)}) copy-start(s32[4,12]{1,0:T(4,128)} %param.38) | copy-start | bytes 580
  11.1 13.3 %copy-start.21 = (s32[48,1]{0,1:T(1,128)S(1)}, s32[48,1]{0,1:T(1,128)}, u32[]{:S(2)}) copy-start(s32[48,1]{0,1:T(1,128)} %param.37) | copy-start | bytes 580
  12.1 18.8 %copy-start.22 = (s32[32]{0:T(128)S(1)}, s32[32]{0:T(128)}, u32[]{:S(2)}) copy-start(s32[32]{0:T(128)} %param.35) | copy-start | bytes 388
  12.1 18.9 %copy-start.23 = (s32[4]{0:T(128)S(1)}, s32[4]{0:T(128)}, u32[]{:S(2)}) copy-start(s32[4]{0:T(128)} %param.36) | copy-start | bytes 52
  12.1 19.1 %copy-start.20 = (s32[4,12]{1,0:T(4,128)S(1)}, s32[4,12]{1,0:T(4,128)}, u32[]{:S(2)}) copy-start(s32[4,12]{1,0:T(4,128)} %param.39) | copy-start | bytes 580
  13.1 128.3 %all-gather.8.cloned.1.call-start = ((), (), s32[]{:S(2)}) async-start(), calls=%async_computation.4 | async-start | bytes 2359296 | tf_op jit(solution)/shard_map/all_gather | solution.py:190
  13.8 177.3 %all-gather.10.cloned.1.call-start = ((), (), s32[]{:S(2)}) async-start(), calls=%async_computation.5 | async-start | bytes 2359296 | tf_op jit(solution)/shard_map/all_gather | solution.py:189
  14.6 285.3 %all-gather.14.cloned.1.call-start = ((), (), s32[]{:S(2)}) async-start(), calls=%async_computation.7 | async-start | bytes 3276800 | tf_op jit(solution)/shard_map/all_gather | solution.py:237
  15.9 22.4 %collective-permute-start = (bf16[384,256]{1,0:T(8,128)(2,1)}, bf16[384,256]{1,0:T(8,128)(2,1)}, u32[]{:S(2)}, u32[]{:S(2)}) collective-permute-start(bf16[384,256]{1,0:T(8,128)(2,1)} %slice.240), channel_id=1, source_target_pairs={{0,4},{4,8},{8,12},{12,16},{16,20},{20,24},{24,28},{1,5},{5,9},{9,... | collective-permute-start | bytes 589832 | tf_op jit(solution)/shard_map/ppermute | solution.py:17
  21.4 18.6 %collective-permute-start.1 = (bf16[384,256]{1,0:T(8,128)(2,1)S(1)}, bf16[384,256]{1,0:T(8,128)(2,1)S(1)}, u32[]{:S(2)}, u32[]{:S(2)}) collective-permute-start(bf16[384,256]{1,0:T(8,128)(2,1)S(1)} %slice.248), channel_id=1, source_target_pairs={{0,4},{4,8},{8,12},{12,16},{16,20},{20,24},{24,28},{1,5},{5,9},{9,... | collective-permute-start | bytes 589832 | tf_op jit(solution)/shard_map/ppermute | solution.py:17
  24.6 0.8 copy-start.13
  25.4 12.2 %all-to-all-start = ((s32[8,1,6]{2,1,0:T(1,128)}), s32[8,1,6]{2,1,0:T(1,128)S(1)}, u32[]{:S(2)}, u32[]{:S(2)}) async-start(s32[8,1,6]{2,1,0:T(1,128)} %bitcast.53), calls=%async_computation | async-start | bytes 8192 | tf_op jit(solution)/shard_map/all_to_all | solution.py:186
  30.2 290.4 %all-gather.12.cloned.1.call-start = ((), (), s32[]{:S(2)}) async-start(), calls=%async_computation.6 | async-start | bytes 7372800 | tf_op jit(solution)/shard_map/all_gather | solution.py:240
  30.8 772.3 %all-reduce.9.cloned.1.call-start = ((), (), s32[]{:S(2)}) async-start(), calls=%async_computation.8 | async-start | bytes 524288 | tf_op jit(solution)/shard_map/psum | solution.py:291
  32.5 59.8 %copy-start.10 = (s32[8]{0:T(128)}, s32[8]{0:T(128)S(1)}, u32[]{:S(2)}) copy-start(s32[8]{0:T(128)S(1)} %eq.130) | copy-start | bytes 100
  355.1 2.5 copy-start
  418.0 2.5 copy-start
  480.9 2.5 copy-start
  544.0 2.5 copy-start
  623.5 7.5 copy-start.9
  651.8 1.0 copy-start.3
  652.8 7.0 copy-start.11
  652.8 9.6 %copy-start.14 = (s32[48]{0:T(128)S(1)}, s32[48]{0:T(128)}, u32[]{:S(2)}) copy-start(s32[48]{0:T(128)} %copy-done.13) | copy-start | bytes 580
  652.8 284.2 %collective-permute-start.2 = (bf16[3,32768]{1,0:T(4,128)(2,1)S(1)}, bf16[3,32768]{1,0:T(4,128)(2,1)}, u32[]{:S(2)}, u32[]{:S(2)}) collective-permute-start(bf16[3,32768]{1,0:T(4,128)(2,1)S(1)} %slice.347), channel_id=1, source_target_pairs={{4,0},{8,4},{12,8},{16,12},{20,16},{24,20},{28,24},{5,1},{9,5},{13... | collective-permute-start | bytes 589832 | tf_op jit(solution)/shard_map/ppermute | solution.py:17
  669.2 5.7 copy-start.8
  669.2 101.3 %all-to-all-start.1 = ((bf16[8,6,32768]{2,1,0:T(8,128)(2,1)}), bf16[8,6,32768]{2,1,0:T(8,128)(2,1)}, u32[]{:S(2)}, u32[]{:S(2)}) async-start(bf16[8,6,32768]{2,1,0:T(8,128)(2,1)} %reshape.496), calls=%async_computation.1 | async-start | bytes 8388608 | tf_op jit(solution)/shard_map/all_to_all | solution.py:314
  674.8 220.7 %all-gather.16.cloned.1.call-start = ((), (), s32[]{:S(2)}) async-start(), calls=%async_computation.9 | async-start | bytes 2359296 | tf_op jit(solution)/shard_map/all_gather | solution.py:106
  676.3 255.6 %reduce-scatter.4.cloned.1.call-start = ((), (), s32[]{:S(2)}) async-start(), calls=%async_computation.10 | async-start | bytes 3276800
  677.5 0.8 copy-start.6
  684.9 4.2 copy-start.7
  684.9 5.5 copy-start.1
  692.1 111.0 %copy-start.17 = (s32[4]{0:T(128)S(1)}, s32[4]{0:T(128)}, u32[]{:S(2)}) copy-start(s32[4]{0:T(128)} %copy-done.16) | copy-start | bytes 52
  692.1 111.0 %copy-start.19 = (f32[4]{0:T(128)S(1)}, f32[4]{0:T(128)}, u32[]{:S(2)}) copy-start(f32[4]{0:T(128)} %copy-done.18) | copy-start | bytes 52
  770.5 169.8 %all-to-all-start.2 = ((bf16[8,6,32768]{2,1,0:T(8,128)(2,1)}), bf16[8,6,32768]{2,1,0:T(8,128)(2,1)}, u32[]{:S(2)}, u32[]{:S(2)}) async-start(bf16[8,6,32768]{2,1,0:T(8,128)(2,1)} %reshape.503), calls=%async_computation.2 | async-start | bytes 8388608 | tf_op jit(solution)/shard_map/all_to_all | solution.py:315
  778.0 154.0 %copy-start.2 = (f32[7,32768]{1,0:T(8,128)}, f32[7,32768]{1,0:T(8,128)S(1)}, u32[]{:S(2)}) copy-start(f32[7,32768]{1,0:T(8,128)S(1)} %scatter-add.29) | copy-start | bytes 2752516
  778.9 164.3 %collective-permute-start.3 = (bf16[3,32768]{1,0:T(4,128)(2,1)}, bf16[3,32768]{1,0:T(4,128)(2,1)}, u32[]{:S(2)}, u32[]{:S(2)}) collective-permute-start(bf16[3,32768]{1,0:T(4,128)(2,1)} %slice.346), channel_id=1, source_target_pairs={{4,0},{8,4},{12,8},{16,12},{20,16},{24,20},{28,24},{5,1},{9,5},{13... | collective-permute-start | bytes 589832 | tf_op jit(solution)/shard_map/ppermute | solution.py:17
  932.0 5.0 copy-start.15
Sparse Core Ops, SparseCore 0:
  13.2 77.6 all-reduce.10
  93.1 48.2 all-gather.7
  143.5 47.6 all-gather.9
  192.6 24.0 all-gather.13
  218.7 101.8 all-gather.11
  662.5 140.5 all-reduce.8
  805.8 89.6 all-gather.15
  898.1 33.8 reduce-scatter.3
